TPU v7x, 32 devices: a whole 2x2x4 slice. The times are simulated.
32 devices in a mesh: groups: 2 (over x), rows: 8 (over z, y), fsdp: 2 (over core).
Axes of the slice: x: 2, y: 2, z: 4, core: 2. Of those that a mesh axis runs over, the one named last changes fastest.
Arguments:
- image: bfloat16 [32, 256, 512], P(('groups', 'rows'), 'fsdp'), parts along dimension 0, may hold values from -81 to 81
- deconv_weight: bfloat16 [4, 4, 512, 256], P(None, None, None, 'fsdp'), may hold values from -0.125 to 0.125
- norm_gain: float32 [256], replicated, may hold values from 0.1 to 1.9
- norm_shift: float32 [256], replicated, may hold values from -3 to 3
- first_weight: bfloat16 [3, 3, 256, 256], P(None, None, None, 'fsdp'), may hold values from -0.125 to 0.125
- first_bias: float32 [256], replicated, may hold values from -3 to 3
- second_weight: bfloat16 [3, 3, 256, 256], P(None, None, None, 'fsdp'), may hold values from -0.125 to 0.125
- second_bias: float32 [256], replicated, may hold values from -3 to 3
Outputs:
- result: bfloat16 [64, 512, 256], P(('groups', 'rows'), 'fsdp'), parts along dimension 0
There are 2 independent parts, one for each index of `groups`. A program takes and returns all parts, laid end to end along the dimension named above; an argument that names none is the same for every part. Nothing has to cross between parts.
All inputs are finite; a program needn't handle non-finite values.
Results may differ from a plain program's by a relative error of at most 0.0055.
Values may be sent and summed in bfloat16 or wider, within the bound.
A program may use at most 64 MiB of HBM per device.

v0:
```python
import functools

import jax
import jax.numpy as jnp
from jax import lax
from jax.experimental import pallas as pl
from jax.experimental.pallas import tpu as pltpu
from jax.sharding import PartitionSpec as P

NORM_GROUPS = 32
EPS = 1e-05
MESH = pl.DeviceIdType.MESH
EDGE = 16
TAPS = ((3, 1), (2, 0))


def silu(v):
    h = 0.5 * v
    return h + h * jnp.tanh(h)


def kernel(
    rows, cores,
    image, dw, gain, shift, w1, b1, w2, b2,
    out,
    xbuf, xf, xs, dwbuf, w1buf, w2buf, up, hf, hs, acts, mix, stats,
    local_sem, send_sem, recv_sem, stat_send, stat_recv, ring,
):
    row, core = lax.axis_index("rows"), lax.axis_index("fsdp")
    other = cores - 1 - core
    count = rows * cores
    me = row * cores + core
    height, breadth, cin = image.shape
    cout = gain.shape[1]
    half = dw.shape[1]
    span = xs.shape[1]
    side = pl.multiple_of(other * (breadth - EDGE), EDGE)
    far = pl.multiple_of(core * (breadth + EDGE), EDGE)
    mine = pl.multiple_of(core * half, 128)

    locals_ = [
        pltpu.make_async_copy(
            image, xbuf.at[pl.ds(height, height), pl.ds(EDGE, breadth)], local_sem.at[0]
        ),
        pltpu.make_async_copy(dw, dwbuf.at[:, pl.ds(mine, half)], local_sem.at[1]),
        pltpu.make_async_copy(w1, w1buf.at[:, pl.ds(mine, half)], local_sem.at[2]),
        pltpu.make_async_copy(w2, w2buf.at[:, pl.ds(mine, half)], local_sem.at[3]),
    ]
    for copy in locals_:
        copy.start()

    barrier = pltpu.get_barrier_semaphore()

    def signal(sem, to_row, to_core):
        pl.semaphore_signal(
            sem, inc=1, device_id={"rows": to_row, "fsdp": to_core}, device_id_type=MESH
        )

    def call(sem, gap, to_cores):
        for inside, to_row in ((row >= gap, row - gap), (row + gap < rows, row + gap)):
            @pl.when(inside)
            def _():
                for to_core in to_cores:
                    signal(sem, to_row, to_core)
        near = jnp.where(row >= gap, 1, 0) + jnp.where(row + gap < rows, 1, 0)
        return near * len(to_cores)

    signal(barrier, row, other)
    met = call(barrier, 1, (core, other)) + 1
    xbuf[:, pl.ds(far, EDGE), :] = jnp.zeros((xbuf.shape[0], EDGE, cin), xbuf.dtype)
    pl.semaphore_wait(barrier, met)

    def remote(src, dst, index, to_row, to_core):
        return pltpu.make_async_remote_copy(
            src_ref=src,
            dst_ref=dst,
            send_sem=send_sem.at[index],
            recv_sem=recv_sem.at[index],
            device_id={"rows": to_row, "fsdp": to_core},
            device_id_type=MESH,
        )

    def piece(src_row, dst_row, index, to_row, low, size):
        return remote(
            image.at[src_row, pl.ds(low, size)],
            xbuf.at[dst_row, pl.ds(EDGE + low, size)],
            index, to_row, core,
        )

    def corner(src_row, dst_row, index, to_row):
        return remote(
            image.at[src_row, pl.ds(side, EDGE)],
            xbuf.at[dst_row, pl.ds(far, EDGE)],
            index, to_row, other,
        )

    below = lax.rem(row + 1, rows)
    above = lax.rem(row + rows - 1, rows)
    to_below = [
        piece(1, 1, 4, below, 0, breadth),
        corner(1, 1, 6, below),
        piece(0, 0, 5, below, 0, breadth),
        corner(0, 0, 7, below),
    ]
    to_above = [
        piece(0, 4, 8, above, 0, breadth),
        corner(0, 4, 10, above),
        piece(1, 5, 9, above, 0, breadth),
        corner(1, 5, 11, above),
    ]
    sides = remote(
        image.at[:, pl.ds(side, EDGE)],
        xbuf.at[pl.ds(height, height), pl.ds(far, EDGE)],
        0, row, other,
    )
    weights = [
        remote(dw, dwbuf.at[:, pl.ds(mine, half)], 1, row, other),
        remote(w1, w1buf.at[:, pl.ds(mine, half)], 2, row, other),
        remote(w2, w2buf.at[:, pl.ds(mine, half)], 3, row, other),
    ]

    def send_halo(part):
        @pl.when(row < rows - 1)
        def _():
            for copy in to_below[part]:
                copy.start()

        @pl.when(row > 0)
        def _():
            for copy in to_above[part]:
                copy.start()

    def take_halo(part):
        @pl.when(row > 0)
        def _():
            for copy in to_below[part]:
                copy.wait_recv()

        @pl.when(row < rows - 1)
        def _():
            for copy in to_above[part]:
                copy.wait_recv()

    send_halo(slice(0, 2))
    sides.start()
    weights[0].start()
    weights[1].start()
    weights[2].start()

    gap, turn = 1, 0
    while gap < rows:
        pl.semaphore_wait(ring.at[turn], call(ring.at[turn], gap, (core,)))
        gap, turn = 2 * gap, turn + 1

    @pl.when(row == 0)
    def _():
        xbuf[pl.ds(0, 2)] = jnp.zeros((2,) + xbuf.shape[1:], xbuf.dtype)

    @pl.when(row == rows - 1)
    def _():
        xbuf[pl.ds(4, 2)] = jnp.zeros((2,) + xbuf.shape[1:], xbuf.dtype)

    def spread_row(r):
        xf[...] = xbuf[r].astype(jnp.float32)
        xs[r, :, pl.ds(0, cin)] = xf[pl.ds(EDGE - 2, span), :].astype(jnp.bfloat16)
        xs[r, :, pl.ds(cin, cin)] = xf[pl.ds(EDGE - 1, span), :].astype(jnp.bfloat16)

    locals_[0].wait()
    sides.wait_recv()
    spread_row(2)
    spread_row(3)

    index = lax.broadcasted_iota(jnp.int32, (span, 1), 0)

    def upsample(pairs, phase_row, phase_col, measure):
        lhs = jnp.concatenate(
            [jnp.concatenate([xs[i], xs[i + 1]], axis=1) for _, i in pairs], axis=0
        )
        rhs = jnp.concatenate(
            [
                dwbuf[pl.ds((TAPS[phase_row][dr] * 4 + TAPS[phase_col][dc]) * cin, cin), :]
                for dr in range(2)
                for dc in range(2)
            ],
            axis=0,
        )
        total = jnp.dot(lhs, rhs, preferred_element_type=jnp.float32).astype(jnp.bfloat16)
        for n, (o, _) in enumerate(pairs):
            block = total[n * span : (n + 1) * span]
            up[o, phase_col] = block
            if measure:
                first = 1 + phase_col
                own = (index >= first) & (index < first + breadth)
                v = jnp.where(own, block.astype(jnp.float32), 0.0)
                stats[me, 0:1] += jnp.sum(v, axis=0, keepdims=True)
                stats[me, 1:2] += jnp.sum(v * v, axis=0, keepdims=True)

    stats[me] = jnp.zeros(stats.shape[1:], stats.dtype)
    locals_[1].wait()
    weights[0].wait_recv()
    for phase_col in range(2):
        upsample(((4, 2),), 0, phase_col, True)
        upsample(((3, 2),), 1, phase_col, True)

    take_halo(slice(0, 2))
    spread_row(1)
    spread_row(4)
    for phase_col in range(2):
        upsample(((2, 1),), 0, phase_col, True)
        upsample(((5, 3),), 1, phase_col, True)

    def stat_copy(slot, peer):
        return pltpu.make_async_remote_copy(
            src_ref=stats.at[me],
            dst_ref=stats.at[me],
            send_sem=stat_send.at[slot],
            recv_sem=stat_recv.at[me],
            device_id={"rows": lax.div(peer, cores), "fsdp": lax.rem(peer, cores)},
            device_id_type=MESH,
        )

    def stat_wait(peer):
        return pltpu.make_async_remote_copy(
            src_ref=stats.at[peer],
            dst_ref=stats.at[peer],
            send_sem=stat_send.at[0],
            recv_sem=stat_recv.at[peer],
            device_id={"rows": lax.div(peer, cores), "fsdp": lax.rem(peer, cores)},
            device_id_type=MESH,
        )

    def send_stats(k, carry):
        stat_copy(k, lax.rem(me + k, count)).start()
        return carry

    lax.fori_loop(1, count, send_stats, 0)
    send_halo(slice(2, 4))
    for phase_col in range(2):
        upsample(((6, 3),), 0, phase_col, False)
        upsample(((1, 1),), 1, phase_col, False)

    def take_stats(k, carry):
        stat_wait(lax.rem(me + k, count)).wait_recv()
        return carry

    lax.fori_loop(1, count, take_stats, 0)

    sums = jnp.sum(stats[...], axis=0)
    width = cout // NORM_GROUPS
    lane_a = lax.broadcasted_iota(jnp.int32, (cout, cout), 0) // width
    lane_b = lax.broadcasted_iota(jnp.int32, (cout, cout), 1) // width
    same = jnp.where(lane_a == lane_b, 1.0, 0.0)
    sums = jnp.dot(
        sums, same, preferred_element_type=jnp.float32, precision=lax.Precision.HIGHEST
    )
    cells = 4 * height * breadth * count * width
    mean = sums[0:1] / cells
    spread = sums[1:2] / cells - mean * mean
    scale = lax.rsqrt(spread + EPS) * gain[...]
    offset = shift[...] - mean * scale

    top, bottom = row == 0, row == rows - 1
    first_col = jnp.where(core == 0, 1, -1)
    last_col = jnp.where(core == cores - 1, breadth, span)
    even_in = (index >= first_col) & (index <= last_col)
    odd_in = (index > first_col) & (index <= last_col + 1)

    def lay(dst, r, even, odd, keep):
        slot = r % 2
        even = jnp.where(even_in & keep, even, 0.0)
        odd = jnp.where(odd_in & keep, odd, 0.0)
        hf[slot, 0, pl.ds(8, span)] = even
        hf[slot, 1, pl.ds(8, span)] = odd
        dst[r, :, pl.ds(0, cout)] = hf[slot, 0, pl.ds(7, span)].astype(jnp.bfloat16)
        dst[r, :, pl.ds(cout, cout)] = odd.astype(jnp.bfloat16)
        dst[r, :, pl.ds(2 * cout, cout)] = even.astype(jnp.bfloat16)
        dst[r, :, pl.ds(3 * cout, cout)] = hf[slot, 1, pl.ds(9, span)].astype(jnp.bfloat16)

    hf[:, :, pl.ds(0, 8)] = jnp.zeros((2, 2, 8, cout), jnp.float32)
    hf[:, :, pl.ds(8 + span, 8)] = jnp.zeros((2, 2, 8, cout), jnp.float32)

    def kept(r, low, high):
        keep = True
        if r < low:
            keep = jnp.logical_not(top)
        if r >= high:
            keep = jnp.logical_not(bottom)
        return keep

    def hide(r):
        even = silu(up[r, 0].astype(jnp.float32) * scale + offset)
        odd = silu(up[r, 1].astype(jnp.float32) * scale + offset)
        lay(hs, r, even, odd, kept(r, 2, 6))

    def convolve(src, lines, weight, bias):
        lhs = jnp.concatenate(
            [
                jnp.concatenate([src[r + a, :, pl.ds(low, 3 * cout)] for a in range(3)], axis=1)
                for r in lines
                for low in (cout, 0)
            ],
            axis=0,
        )
        total = jnp.dot(lhs, weight[...], preferred_element_type=jnp.float32) + bias[...]
        cut = lambda n: total[n * span : (n + 1) * span]
        return [(r, cut(2 * n), cut(2 * n + 1)) for n, r in enumerate(lines)]

    def first(lines):
        for r, even, odd in convolve(hs, lines, w1buf, b1):
            lay(acts, r, silu(even), silu(odd), kept(r, 1, 5))

    def second(lines):
        for r, even, odd in convolve(acts, lines, w2buf, b2):
            for lane in range(cout // 128):
                cut = slice(lane * 128, (lane + 1) * 128)
                mix[r % 2, lane, pl.ds(6, span, stride=2), :] = even[:, cut]
                mix[r % 2, lane, pl.ds(5, span, stride=2), :] = odd[:, cut]
                out[r, :, pl.ds(lane * 128, 128)] = mix[
                    r % 2, lane, pl.ds(8, 2 * breadth), :
                ].astype(jnp.bfloat16)

    for n in range(1, 3):
        locals_[n + 1].wait()
        weights[n].wait_recv()
    for r in range(1, 7):
        hide(r)
    for r in range(1, 5):
        first((r,))

    take_halo(slice(2, 4))
    spread_row(0)
    spread_row(5)
    for phase_col in range(2):
        upsample(((0, 0),), 0, phase_col, False)
        upsample(((7, 4),), 1, phase_col, False)
    hide(0)
    hide(7)
    first((0,))
    first((5,))
    for r in (1, 2, 0, 3):
        second((r,))

    sides.wait_send()
    for copy in weights:
        copy.wait_send()

    @pl.when(row < rows - 1)
    def _():
        for copy in to_below:
            copy.wait_send()

    @pl.when(row > 0)
    def _():
        for copy in to_above:
            copy.wait_send()

    def drain(k, carry):
        stat_copy(k, lax.rem(me + k, count)).wait_send()
        return carry

    lax.fori_loop(1, count, drain, 0)


def local(rows, cores, image, dw, gain, shift, w1, b1, w2, b2):
    height, breadth, cin = image.shape
    half = dw.shape[3]
    cout = gain.shape[0]
    span = breadth + EDGE
    bf16, f32 = jnp.bfloat16, jnp.float32
    count = rows * cores
    vmem = pl.BlockSpec(memory_space=pltpu.VMEM)
    hbm = pl.BlockSpec(memory_space=pl.ANY)
    return pl.pallas_call(
        functools.partial(kernel, rows, cores),
        out_shape=jax.ShapeDtypeStruct((2 * height, 2 * breadth, cout), bf16),
        in_specs=[hbm, hbm, vmem, vmem, hbm, vmem, hbm, vmem],
        out_specs=vmem,
        scratch_shapes=[
            pltpu.VMEM((3 * height, breadth + 2 * EDGE, cin), bf16),
            pltpu.VMEM((breadth + 2 * EDGE, cin), f32),
            pltpu.VMEM((3 * height, span, 2 * cin), bf16),
            pltpu.VMEM((16 * cin, cout), bf16),
            pltpu.VMEM((9 * cout, cout), bf16),
            pltpu.VMEM((9 * cout, cout), bf16),
            pltpu.VMEM((2 * height + 4, 2, span, cout), bf16),
            pltpu.VMEM((2, 2, span + 16, cout), f32),
            pltpu.VMEM((2 * height + 4, span, 4 * cout), bf16),
            pltpu.VMEM((2 * height + 2, span, 4 * cout), bf16),
            pltpu.VMEM((2, cout // 128, 2 * span + 16, 128), f32),
            pltpu.VMEM((count, 2, cout), f32),
            pltpu.SemaphoreType.DMA((4,)),
            pltpu.SemaphoreType.DMA((12,)),
            pltpu.SemaphoreType.DMA((12,)),
            pltpu.SemaphoreType.DMA((count,)),
            pltpu.SemaphoreType.DMA((count,)),
            pltpu.SemaphoreType.REGULAR((max(rows.bit_length(), 1),)),
        ],
        compiler_params=pltpu.CompilerParams(
            collective_id=0, has_side_effects=True, vmem_limit_bytes=60 << 20
        ),
    )(
        image,
        dw.reshape(-1, half),
        gain.reshape(1, -1),
        shift.reshape(1, -1),
        w1.reshape(-1, half),
        b1.reshape(1, -1),
        w2.reshape(-1, half),
        b2.reshape(1, -1),
    )


def solution(mesh):
    placed = (
        P(("groups", "rows"), "fsdp", None),
        P(None, None, None, "fsdp"),
        P(),
        P(),
        P(None, None, None, "fsdp"),
        P(),
        P(None, None, None, "fsdp"),
        P(),
    )
    return jax.shard_map(
        functools.partial(local, mesh.shape["rows"], mesh.shape["fsdp"]),
        mesh=mesh,
        in_specs=placed,
        out_specs=P(("groups", "rows"), "fsdp", None),
        check_vma=False,
    )
```

profile of v0, /device:TPU:0, one launch (start us, length us, event | category | flops | bytes accessed | tf_op | source)
XLA Modules:
  0.0 27.0 jit_solution(10499382172335670466)
XLA Ops:
  0.0 25.1 %shard_map.82 = bf16[4,256,256]{2,1,0:T(8,128)(2,1)} custom-call(bf16[2,128,512]{2,1,0:T(8,128)(2,1)} %image.1, bf16[8192,128]{1,0:T(8,128)(2,1)} %bitcast.7, f32[1,256]{1,0:T(1,128)} %bitcast.10, f32[1,256]{1,0:T(1,128)} %bitcast.11, bf16[2304,128]{1,0:T(8,128)(2,1)} %bitcast.8, f32[1,256]{1,0:T(1,128)} %bitcast.12, bf16[2304,128]{1,0:T(8,128)(2,1)} %bitcast.9, ...), custom_call_target="tpu_custom_call" | custom-call | tf_op jit(solution)/shard_map/pallas_call | solution.py:373
  25.1 1.9 %copy.10 = bf16[4,256,256]{2,1,0:T(8,128)(2,1)} copy(bf16[4,256,256]{2,1,0:T(8,128)(2,1)} %shard_map.82) | data formatting | bytes 1048576
where the time goes:
time: 27.2 us; the launch traced here: 27 us
  Pallas kernels  25.1 us (92%)
  local copies, waits for them, and re-layouts  1.87 us (7%)
    pallas_call x1, Pallas kernels, local(): pl.pallas_call(functools.partial(kernel, rows, cores), out_shape=jax.Shap...  25.1 us
    unnamed x1, local copies, waits for them, and re-layouts  1.87 us

commit v1 on v0

--- a/solution.py
+++ b/solution.py
@@ -21,9 +21,10 @@
 
 def kernel(
     rows, cores,
-    image, dw, gain, shift, w1, b1, w2, b2,
-    out,
-    xbuf, xf, xs, dwbuf, w1buf, w2buf, up, hf, hs, acts, mix, stats,
+    image, dw, gain_in, shift_in, w1, b1_in, w2, b2_in,
+    acts, w2buf, b2,
+    gain, shift, b1,
+    xbuf, xf, xs, dwbuf, w1buf, up, hf, hs, stats, same,
     local_sem, send_sem, recv_sem, stat_send, stat_recv, ring,
 ):
     row, core = lax.axis_index("rows"), lax.axis_index("fsdp")
@@ -45,9 +46,11 @@
         pltpu.make_async_copy(dw, dwbuf.at[:, pl.ds(mine, half)], local_sem.at[1]),
         pltpu.make_async_copy(w1, w1buf.at[:, pl.ds(mine, half)], local_sem.at[2]),
         pltpu.make_async_copy(w2, w2buf.at[:, pl.ds(mine, half)], local_sem.at[3]),
+        pltpu.make_async_copy(gain_in, gain, local_sem.at[4]),
+        pltpu.make_async_copy(shift_in, shift, local_sem.at[5]),
+        pltpu.make_async_copy(b1_in, b1, local_sem.at[6]),
+        pltpu.make_async_copy(b2_in, b2, local_sem.at[7]),
     ]
-    for copy in locals_:
-        copy.start()
 
     barrier = pltpu.get_barrier_semaphore()
 
@@ -67,6 +70,8 @@
 
     signal(barrier, row, other)
     met = call(barrier, 1, (core, other)) + 1
+    for copy in locals_:
+        copy.start()
     xbuf[:, pl.ds(far, EDGE), :] = jnp.zeros((xbuf.shape[0], EDGE, cin), xbuf.dtype)
     pl.semaphore_wait(barrier, met)
 
@@ -94,20 +99,26 @@
             index, to_row, other,
         )
 
-    below = lax.rem(row + 1, rows)
-    above = lax.rem(row + rows - 1, rows)
-    to_below = [
-        piece(1, 1, 4, below, 0, breadth),
-        corner(1, 1, 6, below),
-        piece(0, 0, 5, below, 0, breadth),
-        corner(0, 0, 7, below),
-    ]
-    to_above = [
-        piece(0, 4, 8, above, 0, breadth),
-        corner(0, 4, 10, above),
-        piece(1, 5, 9, above, 0, breadth),
-        corner(1, 5, 11, above),
-    ]
+    top, bottom = row == 0, row == rows - 1
+    below = jnp.where(bottom, row - 1, row + 1)
+    above = jnp.where(top, row + 1, row - 1)
+
+    def pair(src_row, dst_row, index, to_row):
+        return [
+            piece(src_row, dst_row, index, to_row, 0, breadth),
+            corner(src_row, dst_row, index + 1, to_row),
+        ]
+
+    down, up_ = pair(1, 1, 4, below), pair(0, 4, 6, above)
+    last_down, first_up = pair(1, 5, 8, below), pair(0, 0, 10, above)
+    reach = pl.multiple_of(other * EDGE, EDGE)
+
+    def pass_on(src_row, dst_row, index, to_row):
+        line = pl.ds(reach, breadth + EDGE)
+        return remote(xbuf.at[src_row, line], xbuf.at[dst_row, line], index, to_row, core)
+
+    relay_up = pass_on(1, 5, 12, lax.rem(row + rows - 2, rows))
+    relay_down = pass_on(4, 0, 13, lax.rem(row + 2, rows))
     sides = remote(
         image.at[:, pl.ds(side, EDGE)],
         xbuf.at[pl.ds(height, height), pl.ds(far, EDGE)],
@@ -119,38 +130,34 @@
         remote(w2, w2buf.at[:, pl.ds(mine, half)], 3, row, other),
     ]
 
-    def send_halo(part):
-        @pl.when(row < rows - 1)
+    def when(condition, copies, what):
+        @pl.when(condition)
         def _():
-            for copy in to_below[part]:
-                copy.start()
-
-        @pl.when(row > 0)
-        def _():
-            for copy in to_above[part]:
-                copy.start()
-
-    def take_halo(part):
-        @pl.when(row > 0)
-        def _():
-            for copy in to_below[part]:
-                copy.wait_recv()
-
-        @pl.when(row < rows - 1)
-        def _():
-            for copy in to_above[part]:
-                copy.wait_recv()
-
-    send_halo(slice(0, 2))
+            for copy in copies:
+                getattr(copy, what)()
+
+    def send_down():
+        when(jnp.logical_not(bottom), down, "start")
+        when(bottom, last_down, "start")
+
+    def send_up():
+        when(jnp.logical_not(top), up_, "start")
+        when(top, first_up, "start")
+
+    send_down()
     sides.start()
     weights[0].start()
     weights[1].start()
     weights[2].start()
 
-    gap, turn = 1, 0
-    while gap < rows:
-        pl.semaphore_wait(ring.at[turn], call(ring.at[turn], gap, (core,)))
-        gap, turn = 2 * gap, turn + 1
+    gaps = []
+    while (1 << len(gaps)) < rows:
+        gaps.append(1 << len(gaps))
+
+    def meet(turn):
+        pl.semaphore_wait(ring.at[turn], call(ring.at[turn], gaps[turn], (core,)))
+
+    meet(0)
 
     @pl.when(row == 0)
     def _():
@@ -188,26 +195,39 @@
         for n, (o, _) in enumerate(pairs):
             block = total[n * span : (n + 1) * span]
             up[o, phase_col] = block
-            if measure:
+            if measure is not False:
                 first = 1 + phase_col
-                own = (index >= first) & (index < first + breadth)
+                own = (index >= first) & (index < first + breadth) & measure
                 v = jnp.where(own, block.astype(jnp.float32), 0.0)
                 stats[me, 0:1] += jnp.sum(v, axis=0, keepdims=True)
                 stats[me, 1:2] += jnp.sum(v * v, axis=0, keepdims=True)
 
     stats[me] = jnp.zeros(stats.shape[1:], stats.dtype)
+    width = cout // NORM_GROUPS
+    lane_a = lax.broadcasted_iota(jnp.int32, (cout, cout), 0) // width
+    lane_b = lax.broadcasted_iota(jnp.int32, (cout, cout), 1) // width
+    same[...] = jnp.where(lane_a == lane_b, 1.0, 0.0).astype(jnp.bfloat16)
     locals_[1].wait()
     weights[0].wait_recv()
+    send_up()
     for phase_col in range(2):
         upsample(((4, 2),), 0, phase_col, True)
         upsample(((3, 2),), 1, phase_col, True)
 
-    take_halo(slice(0, 2))
+    @pl.when(bottom)
+    def _():
+        spread_row(4)
+        for phase_col in range(2):
+            upsample(((5, 3),), 1, phase_col, True)
+
+    for turn in range(1, len(gaps)):
+        meet(turn)
+
+    when(jnp.logical_not(top), down, "wait_recv")
     spread_row(1)
-    spread_row(4)
     for phase_col in range(2):
         upsample(((2, 1),), 0, phase_col, True)
-        upsample(((5, 3),), 1, phase_col, True)
+        upsample(((1, 1),), 1, phase_col, jnp.logical_not(top))
 
     def stat_copy(slot, peer):
         return pltpu.make_async_remote_copy(
@@ -234,10 +254,17 @@
         return carry
 
     lax.fori_loop(1, count, send_stats, 0)
-    send_halo(slice(2, 4))
+    when(row >= 2, (relay_up,), "start")
+    when(jnp.logical_not(bottom), up_, "wait_recv")
+    when(row + 2 < rows, (relay_down,), "start")
+    spread_row(4)
     for phase_col in range(2):
         upsample(((6, 3),), 0, phase_col, False)
-        upsample(((1, 1),), 1, phase_col, False)
+
+    @pl.when(jnp.logical_not(bottom))
+    def _():
+        for phase_col in range(2):
+            upsample(((5, 3),), 1, phase_col, False)
 
     def take_stats(k, carry):
         stat_wait(lax.rem(me + k, count)).wait_recv()
@@ -246,20 +273,22 @@
     lax.fori_loop(1, count, take_stats, 0)
 
     sums = jnp.sum(stats[...], axis=0)
-    width = cout // NORM_GROUPS
-    lane_a = lax.broadcasted_iota(jnp.int32, (cout, cout), 0) // width
-    lane_b = lax.broadcasted_iota(jnp.int32, (cout, cout), 1) // width
-    same = jnp.where(lane_a == lane_b, 1.0, 0.0)
+    parts = []
+    for _ in range(3):
+        parts.append(sums.astype(jnp.bfloat16))
+        sums = sums - parts[-1].astype(jnp.float32)
     sums = jnp.dot(
-        sums, same, preferred_element_type=jnp.float32, precision=lax.Precision.HIGHEST
+        jnp.concatenate(parts, axis=0), same[...], preferred_element_type=jnp.float32
     )
+    sums = sums[0:2] + sums[2:4] + sums[4:6]
     cells = 4 * height * breadth * count * width
     mean = sums[0:1] / cells
     spread = sums[1:2] / cells - mean * mean
+    for n in range(4, 8):
+        locals_[n].wait()
     scale = lax.rsqrt(spread + EPS) * gain[...]
     offset = shift[...] - mean * scale
 
-    top, bottom = row == 0, row == rows - 1
     first_col = jnp.where(core == 0, 1, -1)
     last_col = jnp.where(core == cores - 1, breadth, span)
     even_in = (index >= first_col) & (index <= last_col)
@@ -309,16 +338,6 @@
         for r, even, odd in convolve(hs, lines, w1buf, b1):
             lay(acts, r, silu(even), silu(odd), kept(r, 1, 5))
 
-    def second(lines):
-        for r, even, odd in convolve(acts, lines, w2buf, b2):
-            for lane in range(cout // 128):
-                cut = slice(lane * 128, (lane + 1) * 128)
-                mix[r % 2, lane, pl.ds(6, span, stride=2), :] = even[:, cut]
-                mix[r % 2, lane, pl.ds(5, span, stride=2), :] = odd[:, cut]
-                out[r, :, pl.ds(lane * 128, 128)] = mix[
-                    r % 2, lane, pl.ds(8, 2 * breadth), :
-                ].astype(jnp.bfloat16)
-
     for n in range(1, 3):
         locals_[n + 1].wait()
         weights[n].wait_recv()
@@ -327,7 +346,10 @@
     for r in range(1, 5):
         first((r,))
 
-    take_halo(slice(2, 4))
+    when(row >= 2, (relay_down,), "wait_recv")
+    when(row == 1, first_up, "wait_recv")
+    when(row + 2 < rows, (relay_up,), "wait_recv")
+    when(row == rows - 2, last_down, "wait_recv")
     spread_row(0)
     spread_row(5)
     for phase_col in range(2):
@@ -337,28 +359,49 @@
     hide(7)
     first((0,))
     first((5,))
-    for r in (1, 2, 0, 3):
-        second((r,))
 
     sides.wait_send()
     for copy in weights:
         copy.wait_send()
-
-    @pl.when(row < rows - 1)
-    def _():
-        for copy in to_below:
-            copy.wait_send()
-
-    @pl.when(row > 0)
-    def _():
-        for copy in to_above:
-            copy.wait_send()
+    when(jnp.logical_not(bottom), down, "wait_send")
+    when(bottom, last_down, "wait_send")
+    when(jnp.logical_not(top), up_, "wait_send")
+    when(top, first_up, "wait_send")
+    when(row >= 2, (relay_up,), "wait_send")
+    when(row + 2 < rows, (relay_down,), "wait_send")
 
     def drain(k, carry):
         stat_copy(k, lax.rem(me + k, count)).wait_send()
         return carry
 
     lax.fori_loop(1, count, drain, 0)
+
+
+def finish(acts, w2buf, b2, out, mix, rows_out, out_sem):
+    span = acts.shape[1]
+    cout = w2buf.shape[1]
+    breadth = span - EDGE
+    copies = []
+    for r in (1, 2, 0, 3):
+        lhs = jnp.concatenate(
+            [
+                jnp.concatenate([acts[r + a, :, pl.ds(low, 3 * cout)] for a in range(3)], axis=1)
+                for low in (cout, 0)
+            ],
+            axis=0,
+        )
+        total = jnp.dot(lhs, w2buf[...], preferred_element_type=jnp.float32) + b2[...]
+        for lane in range(cout // 128):
+            cut = slice(lane * 128, (lane + 1) * 128)
+            mix[r % 2, lane, pl.ds(6, span, stride=2), :] = total[:span, cut]
+            mix[r % 2, lane, pl.ds(5, span, stride=2), :] = total[span:, cut]
+            rows_out[r, :, pl.ds(lane * 128, 128)] = mix[
+                r % 2, lane, pl.ds(8, 2 * breadth), :
+            ].astype(jnp.bfloat16)
+        copies.append(pltpu.make_async_copy(rows_out.at[r], out.at[r], out_sem.at[r]))
+        copies[-1].start()
+    for copy in copies:
+        copy.wait()
 
 
 def local(rows, cores, image, dw, gain, shift, w1, b1, w2, b2):
@@ -369,34 +412,39 @@
     bf16, f32 = jnp.bfloat16, jnp.float32
     count = rows * cores
     vmem = pl.BlockSpec(memory_space=pltpu.VMEM)
-    hbm = pl.BlockSpec(memory_space=pl.ANY)
-    return pl.pallas_call(
+    hbm = pl.BlockSpec(memory_space=pltpu.HBM)
+    acts, w2_whole, b2_kept = pl.pallas_call(
         functools.partial(kernel, rows, cores),
-        out_shape=jax.ShapeDtypeStruct((2 * height, 2 * breadth, cout), bf16),
-        in_specs=[hbm, hbm, vmem, vmem, hbm, vmem, hbm, vmem],
-        out_specs=vmem,
+        out_shape=(
+            pltpu.VMEM((2 * height + 2, span, 4 * cout), bf16),
+            pltpu.VMEM((9 * cout, cout), bf16),
+            pltpu.VMEM((1, cout), f32),
+        ),
+        in_specs=[hbm] * 8,
+        out_specs=(vmem, vmem, vmem),
         scratch_shapes=[
+            pltpu.VMEM((1, cout), f32),
+            pltpu.VMEM((1, cout), f32),
+            pltpu.VMEM((1, cout), f32),
             pltpu.VMEM((3 * height, breadth + 2 * EDGE, cin), bf16),
             pltpu.VMEM((breadth + 2 * EDGE, cin), f32),
             pltpu.VMEM((3 * height, span, 2 * cin), bf16),
             pltpu.VMEM((16 * cin, cout), bf16),
             pltpu.VMEM((9 * cout, cout), bf16),
-            pltpu.VMEM((9 * cout, cout), bf16),
             pltpu.VMEM((2 * height + 4, 2, span, cout), bf16),
             pltpu.VMEM((2, 2, span + 16, cout), f32),
             pltpu.VMEM((2 * height + 4, span, 4 * cout), bf16),
-            pltpu.VMEM((2 * height + 2, span, 4 * cout), bf16),
-            pltpu.VMEM((2, cout // 128, 2 * span + 16, 128), f32),
             pltpu.VMEM((count, 2, cout), f32),
-            pltpu.SemaphoreType.DMA((4,)),
-            pltpu.SemaphoreType.DMA((12,)),
-            pltpu.SemaphoreType.DMA((12,)),
+            pltpu.VMEM((cout, cout), bf16),
+            pltpu.SemaphoreType.DMA((8,)),
+            pltpu.SemaphoreType.DMA((14,)),
+            pltpu.SemaphoreType.DMA((14,)),
             pltpu.SemaphoreType.DMA((count,)),
             pltpu.SemaphoreType.DMA((count,)),
             pltpu.SemaphoreType.REGULAR((max(rows.bit_length(), 1),)),
         ],
         compiler_params=pltpu.CompilerParams(
-            collective_id=0, has_side_effects=True, vmem_limit_bytes=60 << 20
+            collective_id=0, has_side_effects=True, vmem_limit_bytes=61 << 20
         ),
     )(
         image,
@@ -408,6 +456,18 @@
         w2.reshape(-1, half),
         b2.reshape(1, -1),
     )
+    return pl.pallas_call(
+        finish,
+        out_shape=jax.ShapeDtypeStruct((2 * height, 2 * breadth, cout), bf16),
+        in_specs=[vmem, vmem, vmem],
+        out_specs=pl.BlockSpec(memory_space=pl.ANY),
+        scratch_shapes=[
+            pltpu.VMEM((2, cout // 128, 2 * span + 16, 128), f32),
+            pltpu.VMEM((2 * height, 2 * breadth, cout), bf16),
+            pltpu.SemaphoreType.DMA((2 * height,)),
+        ],
+        compiler_params=pltpu.CompilerParams(vmem_limit_bytes=16 << 20),
+    )(acts, w2_whole, b2_kept)
 
 
 def solution(mesh):

time: 27.2 us -> 24.4 us (0.90)
  local copies, waits for them, and re-layouts: 1.87 us -> 0 us
  Pallas kernels: 25.1 us -> 24.2 us
    unnamed x1 -> x0, local copies, waits for them, and re-layouts: 1.87 us -> none
    pallas_call x1 -> x2, Pallas kernels: 25.1 us -> 24.2 us  [the longest x1 21.9 us: local(): pl.pallas_call(functools.partial(kernel, rows, cores), out_shape=(pltpu.V...]
where the time goes in v1:
time: 24.4 us; the launch traced here: 24.2 us
  Pallas kernels  24.2 us (99%)
    pallas_call x1, Pallas kernels, local(): pl.pallas_call(functools.partial(kernel, rows, cores), out_shape=(pltpu.V...  21.9 us
    pallas_call x1, Pallas kernels, local(): pl.pallas_call(finish, out_shape=jax.ShapeDtypeStruct((2 * height, 2 * br...  2.35 us

profile of v1, /device:TPU:0, one launch (start us, length us, event | category | flops | bytes accessed | tf_op | source)
XLA Modules:
  0.0 24.2 jit_solution(10271136188134860038)
XLA Ops:
  0.0 21.9 %shard_map.82 = (bf16[6,144,1024]{2,1,0:T(8,128)(2,1)S(1)}, bf16[2304,256]{1,0:T(8,128)(2,1)S(1)}, f32[1,256]{1,0:T(1,128)S(1)}) custom-call(bf16[2,128,512]{2,1,0:T(8,128)(2,1)} %image.1, bf16[8192,128]{1,0:T(8,128)(2,1)} %bitcast.7, f32[1,256]{1,0:T(1,128)} %bitcast.10, f32[1,256]{1,0:T(1,128)} %bitcast.11, bf16[2304,128]{1,0:T(8,128)(2,1)} %bitcast.8, ...), custom_call_target="tpu_custom_call" | custom-call | tf_op jit(solution)/shard_map/pallas_call | solution.py:416
  21.9 2.4 %shard_map.83 = bf16[4,256,256]{2,1,0:T(8,128)(2,1)} custom-call(bf16[6,144,1024]{2,1,0:T(8,128)(2,1)S(1)} %get-tuple-element.8.acts, bf16[2304,256]{1,0:T(8,128)(2,1)S(1)} %get-tuple-element.9.w2buf, f32[1,256]{1,0:T(1,128)S(1)} %get-tuple-element.10.b2), custom_call_target="tpu_custom_call" | custom-call | tf_op jit(solution)/shard_map/pallas_call | solution.py:459

commit v2 on v1

--- a/solution.py
+++ b/solution.py
@@ -59,21 +59,22 @@
             sem, inc=1, device_id={"rows": to_row, "fsdp": to_core}, device_id_type=MESH
         )
 
+    def near(gap):
+        return jnp.where(row >= gap, 1, 0) + jnp.where(row + gap < rows, 1, 0)
+
     def call(sem, gap, to_cores):
         for inside, to_row in ((row >= gap, row - gap), (row + gap < rows, row + gap)):
             @pl.when(inside)
             def _():
                 for to_core in to_cores:
                     signal(sem, to_row, to_core)
-        near = jnp.where(row >= gap, 1, 0) + jnp.where(row + gap < rows, 1, 0)
-        return near * len(to_cores)
 
     signal(barrier, row, other)
-    met = call(barrier, 1, (core, other)) + 1
+    call(barrier, 1, (core, other))
     for copy in locals_:
         copy.start()
     xbuf[:, pl.ds(far, EDGE), :] = jnp.zeros((xbuf.shape[0], EDGE, cin), xbuf.dtype)
-    pl.semaphore_wait(barrier, met)
+    pl.semaphore_wait(barrier, 2 * near(1) + 1)
 
     def remote(src, dst, index, to_row, to_core):
         return pltpu.make_async_remote_copy(
@@ -103,22 +104,25 @@
     below = jnp.where(bottom, row - 1, row + 1)
     above = jnp.where(top, row + 1, row - 1)
 
-    def pair(src_row, dst_row, index, to_row):
+    def line(src_row, dst_row, index, to_row, sizes):
+        lows = [sum(sizes[:n]) for n in range(len(sizes))]
         return [
-            piece(src_row, dst_row, index, to_row, 0, breadth),
-            corner(src_row, dst_row, index + 1, to_row),
-        ]
-
-    down, up_ = pair(1, 1, 4, below), pair(0, 4, 6, above)
-    last_down, first_up = pair(1, 5, 8, below), pair(0, 0, 10, above)
+            piece(src_row, dst_row, index + 1 + n, to_row, low, size)
+            for n, (low, size) in enumerate(zip(lows, sizes))
+        ] + [corner(src_row, dst_row, index, to_row)]
+
+    early = breadth // 2 // EDGE * EDGE
+    whole, halves = (breadth,), (early, breadth - early)
+    down, up_ = line(1, 1, 4, below, whole), line(0, 4, 6, above, halves)
+    last_down, first_up = line(1, 5, 9, below, whole), line(0, 0, 11, above, halves)
     reach = pl.multiple_of(other * EDGE, EDGE)
 
     def pass_on(src_row, dst_row, index, to_row):
         line = pl.ds(reach, breadth + EDGE)
         return remote(xbuf.at[src_row, line], xbuf.at[dst_row, line], index, to_row, core)
 
-    relay_up = pass_on(1, 5, 12, lax.rem(row + rows - 2, rows))
-    relay_down = pass_on(4, 0, 13, lax.rem(row + 2, rows))
+    relay_up = pass_on(1, 5, 14, lax.rem(row + rows - 2, rows))
+    relay_down = pass_on(4, 0, 15, lax.rem(row + 2, rows))
     sides = remote(
         image.at[:, pl.ds(side, EDGE)],
         xbuf.at[pl.ds(height, height), pl.ds(far, EDGE)],
@@ -140,9 +144,9 @@
         when(jnp.logical_not(bottom), down, "start")
         when(bottom, last_down, "start")
 
-    def send_up():
-        when(jnp.logical_not(top), up_, "start")
-        when(top, first_up, "start")
+    def send_up(part):
+        when(jnp.logical_not(top), up_[part], "start")
+        when(top, first_up[part], "start")
 
     send_down()
     sides.start()
@@ -155,7 +159,10 @@
         gaps.append(1 << len(gaps))
 
     def meet(turn):
-        pl.semaphore_wait(ring.at[turn], call(ring.at[turn], gaps[turn], (core,)))
+        if turn:
+            pl.semaphore_wait(ring.at[turn - 1], near(gaps[turn - 1]))
+        if turn < len(gaps):
+            call(ring.at[turn], gaps[turn], (core,))
 
     meet(0)
 
@@ -172,6 +179,7 @@
         xs[r, :, pl.ds(0, cin)] = xf[pl.ds(EDGE - 2, span), :].astype(jnp.bfloat16)
         xs[r, :, pl.ds(cin, cin)] = xf[pl.ds(EDGE - 1, span), :].astype(jnp.bfloat16)
 
+    meet(1)
     locals_[0].wait()
     sides.wait_recv()
     spread_row(2)
@@ -207,9 +215,11 @@
     lane_a = lax.broadcasted_iota(jnp.int32, (cout, cout), 0) // width
     lane_b = lax.broadcasted_iota(jnp.int32, (cout, cout), 1) // width
     same[...] = jnp.where(lane_a == lane_b, 1.0, 0.0).astype(jnp.bfloat16)
+    for turn in range(2, len(gaps)):
+        meet(turn)
+    send_up(slice(0, 1))
     locals_[1].wait()
     weights[0].wait_recv()
-    send_up()
     for phase_col in range(2):
         upsample(((4, 2),), 0, phase_col, True)
         upsample(((3, 2),), 1, phase_col, True)
@@ -219,9 +229,6 @@
         spread_row(4)
         for phase_col in range(2):
             upsample(((5, 3),), 1, phase_col, True)
-
-    for turn in range(1, len(gaps)):
-        meet(turn)
 
     when(jnp.logical_not(top), down, "wait_recv")
     spread_row(1)
@@ -253,7 +260,10 @@
         stat_copy(k, lax.rem(me + k, count)).start()
         return carry
 
+    for turn in range(max(2, len(gaps)), len(gaps) + 1):
+        meet(turn)
     lax.fori_loop(1, count, send_stats, 0)
+    send_up(slice(1, 3))
     when(row >= 2, (relay_up,), "start")
     when(jnp.logical_not(bottom), up_, "wait_recv")
     when(row + 2 < rows, (relay_down,), "start")
@@ -437,8 +447,8 @@
             pltpu.VMEM((count, 2, cout), f32),
             pltpu.VMEM((cout, cout), bf16),
             pltpu.SemaphoreType.DMA((8,)),
-            pltpu.SemaphoreType.DMA((14,)),
-            pltpu.SemaphoreType.DMA((14,)),
+            pltpu.SemaphoreType.DMA((16,)),
+            pltpu.SemaphoreType.DMA((16,)),
             pltpu.SemaphoreType.DMA((count,)),
             pltpu.SemaphoreType.DMA((count,)),
             pltpu.SemaphoreType.REGULAR((max(rows.bit_length(), 1),)),

time: 24.4 us -> 23.1 us (0.947)
  Pallas kernels: 24.2 us -> 23 us
    pallas_call x1, Pallas kernels: 21.9 us -> 20.6 us  [local(): pl.pallas_call(functools.partial(kernel, rows, cores), out_shape=(pltpu.V...]
where the time goes in v2:
time: 23.1 us; the launch traced here: 23 us
  Pallas kernels  23 us (100%)
    pallas_call x1, Pallas kernels, local(): pl.pallas_call(functools.partial(kernel, rows, cores), out_shape=(pltpu.V...  20.6 us
    pallas_call x1, Pallas kernels, local(): pl.pallas_call(finish, out_shape=jax.ShapeDtypeStruct((2 * height, 2 * br...  2.35 us

profile of v2, /device:TPU:0, one launch (start us, length us, event | category | flops | bytes accessed | tf_op | source)
XLA Modules:
  0.0 23.0 jit_solution(14291729217163312692)
XLA Ops:
  0.0 20.6 %shard_map.82 = (bf16[6,144,1024]{2,1,0:T(8,128)(2,1)S(1)}, bf16[2304,256]{1,0:T(8,128)(2,1)S(1)}, f32[1,256]{1,0:T(1,128)S(1)}) custom-call(bf16[2,128,512]{2,1,0:T(8,128)(2,1)} %image.1, bf16[8192,128]{1,0:T(8,128)(2,1)} %bitcast.7, f32[1,256]{1,0:T(1,128)} %bitcast.10, f32[1,256]{1,0:T(1,128)} %bitcast.11, bf16[2304,128]{1,0:T(8,128)(2,1)} %bitcast.8, ...), custom_call_target="tpu_custom_call" | custom-call | tf_op jit(solution)/shard_map/pallas_call | solution.py:426
  20.6 2.4 %shard_map.83 = bf16[4,256,256]{2,1,0:T(8,128)(2,1)} custom-call(bf16[6,144,1024]{2,1,0:T(8,128)(2,1)S(1)} %get-tuple-element.8.acts, bf16[2304,256]{1,0:T(8,128)(2,1)S(1)} %get-tuple-element.9.w2buf, f32[1,256]{1,0:T(1,128)S(1)} %get-tuple-element.10.b2), custom_call_target="tpu_custom_call" | custom-call | tf_op jit(solution)/shard_map/pallas_call | solution.py:469
